TPU v7x, 512 devices: a whole 4x8x8 slice. The times are simulated.
512 devices in a mesh: doc: 16 (over z, core), gram: 32 (over x, y).
Axes of the slice: x: 4, y: 8, z: 8, core: 2. Of those that a mesh axis runs over, the one named last changes fastest.
Arguments:
- w_factor: bfloat16 [24576, 256], P(('doc', 'gram')), may hold values from 0.003 to 0.1
- h_factor: bfloat16 [49152, 256], P(('gram', 'doc')), may hold values from 0.003 to 0.1
- tile_counts: bfloat16 [16, 32, 24, 128, 128], P('doc', 'gram'), may hold values from 0 to 30, as said below
- tile_rows: int32 [16, 32, 24], P('doc', 'gram'), may hold values from 0 to 11, as said below
- tile_cols: int32 [16, 32, 24], P('doc', 'gram'), may hold values from 0 to 11, as said below
- tile_live: int32 [16, 32], P('doc', 'gram'), may hold values from 1 to 24, as said below
Outputs:
- w_next: bfloat16 [24576, 256], P(('doc', 'gram'))
- h_next: bfloat16 [49152, 256], P(('gram', 'doc'))
Inputs may be any that keep to these rules, and one draw needn't show every extreme that they name: `tile_rows`: within one device pair the first tile_live slots name distinct tiles; slots hold positions in every case. `tile_cols`: see tile_rows. `tile_live`: some device pair holds 24 tiles. `tile_counts`: whole numbers.
All inputs are finite; a program needn't handle non-finite values.
Results may differ from a plain program's by a relative error of at most 0.0021.
Values may be sent and summed in bfloat16 or wider, within the bound.
A program may use at most 64 MiB of HBM per device.

v0:
```python
import jax
import jax.numpy as jnp
from jax import lax
from jax.sharding import PartitionSpec as P

GROUP = 8


def group_terms(w_tiles, h_tiles, rows, cols, counts, keep):
    wt = jnp.take(w_tiles, rows, axis=0)
    ht = jnp.take(h_tiles, cols, axis=0)
    model = jnp.einsum("spk,sqk->spq", wt, ht, preferred_element_type=jnp.float32)
    ratio = (counts.astype(jnp.float32) / model * keep[:, None, None]).astype(jnp.bfloat16)
    w_part = jnp.einsum("spq,sqk->spk", ratio, ht, preferred_element_type=jnp.float32)
    h_part = jnp.einsum("spq,spk->sqk", ratio, wt, preferred_element_type=jnp.float32)
    pick_r = (rows[:, None] == jnp.arange(w_tiles.shape[0], dtype=jnp.int32)[None, :]).astype(
        jnp.float32
    )
    pick_c = (cols[:, None] == jnp.arange(h_tiles.shape[0], dtype=jnp.int32)[None, :]).astype(
        jnp.float32
    )
    add_w = jnp.einsum("st,spk->tpk", pick_r, w_part, precision=lax.Precision.HIGHEST)
    add_h = jnp.einsum("st,spk->tpk", pick_c, h_part, precision=lax.Precision.HIGHEST)
    return (add_w, add_h)


def body(w_factor, h_factor, tile_counts, tile_rows, tile_cols, tile_live):
    topics = w_factor.shape[1]
    w_block = lax.all_gather(w_factor, "gram", axis=0, tiled=True)
    h_block = lax.all_gather(h_factor, "doc", axis=0, tiled=True)
    tile_side = tile_counts.shape[3]
    w_tiles = w_block.reshape(-1, tile_side, topics)
    h_tiles = h_block.reshape(-1, tile_side, topics)
    rows = tile_rows[0, 0]
    cols = tile_cols[0, 0]
    counts = tile_counts[0, 0]
    live = tile_live[0, 0]
    slots = rows.shape[0]
    width = GROUP
    start = (jnp.zeros(w_tiles.shape, jnp.float32), jnp.zeros(h_tiles.shape, jnp.float32))
    steps = slots // width
    marks = (jnp.arange(slots, dtype=jnp.int32) < live).astype(jnp.float32)

    def visit(carry, pieces):
        part_rows, part_cols, part_counts, part_keep = pieces
        add_w, add_h = group_terms(w_tiles, h_tiles, part_rows, part_cols, part_counts, part_keep)
        return ((carry[0] + add_w, carry[1] + add_h), None)

    pieces = (
        rows.reshape(steps, width),
        cols.reshape(steps, width),
        counts.reshape(steps, width, tile_side, tile_side),
        marks.reshape(steps, width),
    )
    (w_numer, h_numer), _ = lax.scan(visit, start, pieces)
    flat_w = w_numer.reshape(-1, topics)
    flat_h = h_numer.reshape(-1, topics)
    w_rows = w_factor.shape[0]
    h_rows = h_factor.shape[0]
    summed_w = lax.psum(flat_w, "gram")
    share_w = lax.dynamic_slice_in_dim(summed_w, lax.axis_index("gram") * w_rows, w_rows, 0)
    summed_h = lax.psum(flat_h, "doc")
    share_h = lax.dynamic_slice_in_dim(summed_h, lax.axis_index("doc") * h_rows, h_rows, 0)
    h_sums = jnp.sum(h_factor.astype(jnp.float32), axis=0)
    w_sums = jnp.sum(w_factor.astype(jnp.float32), axis=0)
    w_denom, h_denom = lax.psum((h_sums, w_sums), ("doc", "gram"))
    w_next = (w_factor.astype(jnp.float32) * share_w / w_denom).astype(jnp.bfloat16)
    h_next = (h_factor.astype(jnp.float32) * share_h / h_denom).astype(jnp.bfloat16)
    return (w_next, h_next)


def solution(mesh):
    in_specs = (
        P(("doc", "gram"), None),
        P(("gram", "doc"), None),
        P("doc", "gram", None, None, None),
        P("doc", "gram", None),
        P("doc", "gram", None),
        P("doc", "gram"),
    )
    out_specs = (P(("doc", "gram"), None), P(("gram", "doc"), None))
    return jax.shard_map(body, mesh=mesh, in_specs=in_specs, out_specs=out_specs, check_vma=False)
```

profile of v0, /device:TPU:64, one launch (start us, length us, event | category | flops | bytes accessed | tf_op | source)
XLA Modules:
  0.0 419.8 jit_solution(2480098275050584792)
XLA Ops:
  9.1 50.8 %all_gather.6 = bf16[1536,256]{1,0:T(8,128)(2,1)S(1)} all-gather(bf16[48,256]{1,0:T(8,128)(2,1)} %param.10), channel_id=1, replica_groups=mesh['doc'=16,'gram'=32] {'gram'}, dimensions={0}, use_global_device_ids=true | all-gather | bytes 811008 | tf_op jit(solution)/shard_map/all_gather | solution.py:29
  61.4 23.9 %all_gather.7 = bf16[1536,256]{1,0:T(8,128)(2,1)} all-gather(bf16[96,256]{1,0:T(8,128)(2,1)} %param.11), channel_id=1, replica_groups=mesh['doc'=16,'gram'=32] {'doc'}, dimensions={0}, use_global_device_ids=true | all-gather | bytes 835584 | tf_op jit(solution)/shard_map/all_gather | solution.py:30
  85.9 38.7 %while.13 = (s32[]{:T(128)}, f32[12,128,256]{2,0,1:T(8,128)S(1)}, f32[12,128,256]{2,0,1:T(8,128)}, s32[3,8]{1,0:T(4,128)S(1)}, bf16[3,8,128,128]{3,2,1,0:T(8,128...) while((s32[]{:T(128)}, f32[12,128,256]{2,0,1:T(8,128)S(1)}, ...), condition=%wide.region_1.3_spmd.clone, body=%wide.region_0.2_spmd.clone.sunk | while | flops 279972160 | bytes 40903584 | solution.py:55
  86.8 1.7 gather_fusion.1
  89.3 1.3 fusion.44
  90.7 1.4 fusion.45
  92.1 2.5 select_add_fusion.4
  95.0 2.5 select_add_fusion.5
  97.5 1.3 copy-done.1
  99.7 1.7 gather_fusion.1
  103.6 1.4 fusion.45
  105.0 2.5 select_add_fusion.4
  107.9 2.5 select_add_fusion.5
  112.6 1.7 gather_fusion.1
  116.5 1.4 fusion.45
  117.9 2.5 select_add_fusion.4
  120.8 2.5 select_add_fusion.5
  124.6 3.7 copy.9
  128.4 2.1 copy.8
  130.6 96.5 %all-reduce = (f32[256]{0:T(256)S(1)}, f32[256]{0:T(256)S(1)}) all-reduce(f32[256]{0:T(256)S(1)} %convert_reduce_fusion, f32[256]{0:T(256)S(1)} %convert_reduce_fusion.1), channel_id=1, replica_groups=mesh['doc'=16,'gram'=32] {'doc','gram'}, use_global_device_ids=true, to_apply=%region_4.6 | all-reduce | flops 512 | bytes 4096 | tf_op jit(solution)/shard_map/psum | solution.py:66
  227.1 15.2 %all-reduce.6.cloned.1.call-done = f32[1536,256]{1,0:T(8,128)} async-done(((f32[1536,256]{1,0:T(8,128)}), f32[1536,256]{1,0:T(8,128)}) %all-reduce.6.cloned.1.call-update) | async-done | bytes 1572880 | tf_op jit(solution)/shard_map/psum | solution.py:62
  242.3 1.5 fusion.19
  243.8 167.7 %all-reduce.4.cloned.1.call-done = f32[1536,256]{1,0:T(8,128)} async-done(((f32[1536,256]{1,0:T(8,128)}), f32[1536,256]{1,0:T(8,128)}) %all-reduce.4.cloned.1.call-update) | async-done | bytes 1572880 | tf_op jit(solution)/shard_map/psum | solution.py:60
  411.6 1.4 fusion.21
  (85 shorter events, 14.8 us)
Async XLA Ops:
  7.2 235.2 %all-reduce.6.cloned.1.call-start = ((), (), s32[]{:S(2)}) async-start(), calls=%async_computation.1 | async-start | bytes 3145728 | tf_op jit(solution)/shard_map/psum | solution.py:62
  85.9 0.9 copy-start.5
  86.6 2.0 copy-start.2
  88.5 0.8 copy-start.4
  92.1 2.5 copy-start.3
  92.1 2.9 copy-start
  95.0 3.8 copy-start.6
  97.5 1.4 copy-start.1
  98.8 0.9 copy-start.5
  99.5 2.0 copy-start.2
  101.4 0.8 copy-start.4
  105.0 2.5 copy-start.3
  105.0 2.9 copy-start
  107.9 3.8 copy-start.6
  110.4 1.4 copy-start.1
  111.7 0.9 copy-start.5
  112.4 2.0 copy-start.2
  117.9 2.5 copy-start.3
  117.9 2.9 copy-start
  120.8 3.8 copy-start.6
  123.3 1.4 copy-start.1
  128.3 283.3 %all-reduce.4.cloned.1.call-start = ((), (), s32[]{:S(2)}) async-start(), calls=%async_computation | async-start | bytes 3145728 | tf_op jit(solution)/shard_map/psum | solution.py:60
  128.4 2.2 copy-start.8
  128.4 2.2 copy-start.7
  (1 other events, 0.8 us)
Sparse Core Ops, SparseCore 0:
  128.4 113.8 all-reduce.5
  245.7 165.8 all-reduce.3
where the time goes:
time: 421 us; the launch traced here: 420 us
  waiting for transfers between devices  183 us (43%)
  blocking collectives  171 us (41%)
  matrix products  24.2 us (6%)
  local copies, waits for them, and re-layouts  20.4 us (5%)
  between operations  14.8 us (4%)
  other arithmetic  5.76 us (1%)
    psum x1, waiting for transfers between devices, body(): summed_w = lax.psum(flat_w, 'gram')  168 us
    psum x1, blocking collectives, body(): w_denom, h_denom = lax.psum((h_sums, w_sums), ('doc', 'gram'))  96.5 us
    all_gather x1, blocking collectives, body(): w_block = lax.all_gather(w_factor, 'gram', axis=0, tiled=True)  50.8 us
    all_gather x1, blocking collectives, body(): h_block = lax.all_gather(h_factor, 'doc', axis=0, tiled=True)  23.9 us
    psum x1, waiting for transfers between devices, body(): summed_h = lax.psum(flat_h, 'doc')  15.2 us
  transfers between devices with their start and end apart: 2, of which 2 were waited for; matrix products, arithmetic and copies ran while one was open for 1% of the time, Pallas kernels for 0%

commit v1 on v0

--- a/solution.py
+++ b/solution.py
@@ -57,7 +57,11 @@
     flat_h = h_numer.reshape(-1, topics)
     w_rows = w_factor.shape[0]
     h_rows = h_factor.shape[0]
-    summed_w = lax.psum(flat_w, "gram")
+    summed_w = flat_w
+    for hop in (1, 2, 4, 8, 16):
+        summed_w = summed_w + lax.ppermute(
+            summed_w, "gram", [(dev, dev ^ hop) for dev in range(32)]
+        )
     share_w = lax.dynamic_slice_in_dim(summed_w, lax.axis_index("gram") * w_rows, w_rows, 0)
     summed_h = lax.psum(flat_h, "doc")
     share_h = lax.dynamic_slice_in_dim(summed_h, lax.axis_index("doc") * h_rows, h_rows, 0)

time: 421 us -> 485 us (1.15)
  the two profiles are of different devices: /device:TPU:64 before, /device:TPU:1 now
where the time goes in v1:
time: 485 us; the launch traced here: 484 us
  waiting for transfers between devices  226 us (47%)
  blocking collectives  175 us (36%)
  matrix products  27.1 us (6%)
  starting transfers between devices  20 us (4%)
  between operations  14.8 us (3%)
  local copies, waits for them, and re-layouts  13.6 us (3%)
  other arithmetic  7.73 us (2%)
    ppermute x5, waiting for transfers between devices, body(): lax.ppermute(summed_w, 'gram', [(dev, dev ^ hop) for dev in range(32)])  207 us
    psum x1, blocking collectives, body(): w_denom, h_denom = lax.psum((h_sums, w_sums), ('doc', 'gram'))  95.5 us
    all_gather x1, blocking collectives, body(): w_block = lax.all_gather(w_factor, 'gram', axis=0, tiled=True)  40.1 us
    all_gather x1, blocking collectives, body(): h_block = lax.all_gather(h_factor, 'doc', axis=0, tiled=True)  39.1 us
    ppermute x5, starting transfers between devices, body(): lax.ppermute(summed_w, 'gram', [(dev, dev ^ hop) for dev in range(32)])  20 us
    psum x1, waiting for transfers between devices, body(): summed_h = lax.psum(flat_h, 'doc')  18.4 us
    dot_general x3, matrix products, group_terms(): jnp.einsum('st,spk->tpk', pick_c, h_part, precision=lax.Precision.HIGHEST)  10.3 us
  transfers between devices with their start and end apart: 6, of which 5 were waited for; matrix products, arithmetic and copies ran while one was open for 1% of the time, Pallas kernels for 0%

profile of v1, /device:TPU:1, one launch (start us, length us, event | category | flops | bytes accessed | tf_op | source)
XLA Modules:
  0.0 484.1 jit_solution(17755318739330288574)
XLA Ops:
  10.5 40.1 %all_gather.6 = bf16[1536,256]{1,0:T(8,128)(2,1)S(1)} all-gather(bf16[48,256]{1,0:T(8,128)(2,1)} %param.10), channel_id=1, replica_groups=mesh['doc'=16,'gram'=32] {'gram'}, dimensions={0}, use_global_device_ids=true | all-gather | bytes 811008 | tf_op jit(solution)/shard_map/all_gather | solution.py:29
  50.6 39.1 %all_gather.7 = bf16[1536,256]{1,0:T(8,128)(2,1)} all-gather(bf16[96,256]{1,0:T(8,128)(2,1)} %param.11), channel_id=1, replica_groups=mesh['doc'=16,'gram'=32] {'doc'}, dimensions={0}, use_global_device_ids=true | all-gather | bytes 835584 | tf_op jit(solution)/shard_map/all_gather | solution.py:30
  90.3 37.5 %while.13 = (s32[]{:T(128)}, f32[12,128,256]{2,0,1:T(8,128)S(1)}, f32[12,128,256]{2,0,1:T(8,128)}, s32[3,8]{1,0:T(4,128)S(1)}, bf16[3,8,128,128]{3,2,1,0:T(8,128...) while((s32[]{:T(128)}, f32[12,128,256]{2,0,1:T(8,128)S(1)}, ...), condition=%wide.region_1.3_spmd.clone, body=%wide.region_0.2_spmd.clone.sunk | while | flops 279972160 | bytes 28320608 | solution.py:55
  91.2 1.7 gather_fusion.1
  96.5 2.6 select_add_fusion.5
  99.5 2.5 select_add_fusion.4
  102.9 1.7 gather_fusion.1
  108.2 3.9 select_add_fusion.5
  112.4 2.5 select_add_fusion.4
  115.8 1.7 gather_fusion.1
  121.1 3.9 select_add_fusion.5
  125.3 2.5 select_add_fusion.4
  128.8 2.4 collective-permute-start
  131.2 35.3 %collective-permute-done = f32[1536,256]{1,0:T(8,128)S(1)} collective-permute-done((f32[1536,256]{1,0:T(8,128)S(1)}, f32[1536,256]{1,0:T(8,128)S(1)}, u32[]{:S(2)}, u32[]{:S(2)}) %collective-permute-start) | collective-permute-done | bytes 1572896 | tf_op jit(solution)/shard_map/ppermute | solution.py:62
  166.6 3.6 collective-permute-start.1
  170.3 68.9 %collective-permute-done.1 = f32[1536,256]{1,0:T(8,128)S(1)} collective-permute-done((f32[1536,256]{1,0:T(8,128)S(1)}, f32[1536,256]{1,0:T(8,128)S(1)}, u32[]{:S(2)}, u32[]{:S(2)}) %collective-permute-start.1) | collective-permute-done | bytes 1572896 | tf_op jit(solution)/shard_map/ppermute | solution.py:62
  239.5 6.0 %collective-permute-start.2 = (f32[1536,256]{1,0:T(8,128)S(1)}, f32[1536,256]{1,0:T(8,128)S(1)}, u32[]{:S(2)}, u32[]{:S(2)}) collective-permute-start(f32[1536,256]{1,0:T(8,128)S(1)} %add.41), channel_id=1, source_target_pairs={{0,4},{1,5},{2,6},{3,7},{4,0},{5,1},{6,2},{7,3},{8,12},{9,13},{10,... | collective-permute-start | bytes 4718600 | tf_op jit(solution)/shard_map/ppermute | solution.py:62
  245.4 69.1 %collective-permute-done.2 = f32[1536,256]{1,0:T(8,128)S(1)} collective-permute-done((f32[1536,256]{1,0:T(8,128)S(1)}, f32[1536,256]{1,0:T(8,128)S(1)}, u32[]{:S(2)}, u32[]{:S(2)}) %collective-permute-start.2) | collective-permute-done | bytes 1572896 | tf_op jit(solution)/shard_map/ppermute | solution.py:62
  314.8 2.5 collective-permute-start.3
  317.3 34.0 %collective-permute-done.3 = f32[1536,256]{1,0:T(8,128)S(1)} collective-permute-done((f32[1536,256]{1,0:T(8,128)S(1)}, f32[1536,256]{1,0:T(8,128)S(1)}, u32[]{:S(2)}, u32[]{:S(2)}) %collective-permute-start.3) | collective-permute-done | bytes 1572896 | tf_op jit(solution)/shard_map/ppermute | solution.py:62
  352.6 5.5 %collective-permute-start.4 = (f32[1536,256]{1,0:T(8,128)}, f32[1536,256]{1,0:T(8,128)}, u32[]{:S(2)}, u32[]{:S(2)}) collective-permute-start(f32[1536,256]{1,0:T(8,128)} %add.43), channel_id=1, source_target_pairs={{0,16},{1,17},{2,18},{3,19},{4,20},{5,21},{6,22},{7,23},{8,24},{9,... | collective-permute-start | bytes 4718600 | tf_op jit(solution)/shard_map/ppermute | solution.py:62
  358.1 2.1 copy.9
  360.4 95.5 %all-reduce = (f32[256]{0:T(256)S(1)}, f32[256]{0:T(256)S(1)}) all-reduce(f32[256]{0:T(256)S(1)} %convert_reduce_fusion, f32[256]{0:T(256)S(1)} %convert_reduce_fusion.1), channel_id=1, replica_groups=mesh['doc'=16,'gram'=32] {'doc','gram'}, use_global_device_ids=true, to_apply=%region_3.5 | all-reduce | flops 512 | bytes 4096 | tf_op jit(solution)/shard_map/psum | solution.py:70
  455.9 18.4 %all-reduce.3.cloned.1.call-done = f32[1536,256]{1,0:T(8,128)} async-done(((f32[1536,256]{1,0:T(8,128)}), f32[1536,256]{1,0:T(8,128)}) %all-reduce.3.cloned.1.call-update) | async-done | bytes 1572880 | tf_op jit(solution)/shard_map/psum | solution.py:66
  (86 shorter events, 23.4 us)
Async XLA Ops:
  7.2 467.1 %all-reduce.3.cloned.1.call-start = ((), (), s32[]{:S(2)}) async-start(), calls=%async_computation | async-start | bytes 3145728 | tf_op jit(solution)/shard_map/psum | solution.py:66
  90.3 0.9 copy-start.4
  91.0 2.0 copy-start.3
  92.9 0.8 copy-start.1
  96.5 2.6 copy-start.2
  99.5 2.5 copy-start.5
  102.0 0.9 copy-start.4
  102.7 2.0 copy-start.3
  104.6 0.8 copy-start.1
  108.2 3.9 copy-start.2
  112.4 2.5 copy-start.5
  114.9 0.9 copy-start.4
  115.6 2.0 copy-start.3
  117.5 0.8 copy-start.1
  121.1 3.9 copy-start.2
  125.3 2.5 copy-start.5
  128.8 37.7 %collective-permute-start = (f32[1536,256]{1,0:T(8,128)S(1)}, f32[1536,256]{1,0:T(8,128)S(1)}, u32[]{:S(2)}, u32[]{:S(2)}) collective-permute-start(f32[1536,256]{1,0:T(8,128)S(1)} %bitcast.42), channel_id=1, source_target_pairs={{0,1},{1,0},{2,3},{3,2},{4,5},{5,4},{6,7},{7,6},{8,9},{9,8},{10,11... | collective-permute-start | bytes 4718600 | tf_op jit(solution)/shard_map/ppermute | solution.py:62
  166.6 72.6 %collective-permute-start.1 = (f32[1536,256]{1,0:T(8,128)S(1)}, f32[1536,256]{1,0:T(8,128)S(1)}, u32[]{:S(2)}, u32[]{:S(2)}) collective-permute-start(f32[1536,256]{1,0:T(8,128)S(1)} %bitcast_add_fusion), channel_id=1, source_target_pairs={{0,2},{1,3},{2,0},{3,1},{4,6},{5,7},{6,4},{7,5},{8,10},{9,11},{10,... | collective-permute-start | bytes 4718600 | tf_op jit(solution)/shard_map/ppermute | solution.py:62
  239.5 75.1 %collective-permute-start.2 = (f32[1536,256]{1,0:T(8,128)S(1)}, f32[1536,256]{1,0:T(8,128)S(1)}, u32[]{:S(2)}, u32[]{:S(2)}) collective-permute-start(f32[1536,256]{1,0:T(8,128)S(1)} %add.41), channel_id=1, source_target_pairs={{0,4},{1,5},{2,6},{3,7},{4,0},{5,1},{6,2},{7,3},{8,12},{9,13},{10,... | collective-permute-start | bytes 4718600 | tf_op jit(solution)/shard_map/ppermute | solution.py:62
  314.8 43.4 %copy-start = (f32[12,128,256]{2,0,1:T(8,128)S(1)}, f32[12,128,256]{2,0,1:T(8,128)}, u32[]{:S(2)}) copy-start(f32[12,128,256]{2,0,1:T(8,128)} %get-tuple-element.52) | copy-start | bytes 4718596
  314.8 36.5 %collective-permute-start.3 = (f32[1536,256]{1,0:T(8,128)S(1)}, f32[1536,256]{1,0:T(8,128)S(1)}, u32[]{:S(2)}, u32[]{:S(2)}) collective-permute-start(f32[1536,256]{1,0:T(8,128)S(1)} %add.42), channel_id=1, source_target_pairs={{0,8},{1,9},{2,10},{3,11},{4,12},{5,13},{6,14},{7,15},{8,0},{9,1},... | collective-permute-start | bytes 4718600 | tf_op jit(solution)/shard_map/ppermute | solution.py:62
  352.6 123.2 %collective-permute-start.4 = (f32[1536,256]{1,0:T(8,128)}, f32[1536,256]{1,0:T(8,128)}, u32[]{:S(2)}, u32[]{:S(2)}) collective-permute-start(f32[1536,256]{1,0:T(8,128)} %add.43), channel_id=1, source_target_pairs={{0,16},{1,17},{2,18},{3,19},{4,20},{5,21},{6,22},{7,23},{8,24},{9,... | collective-permute-start | bytes 4718600 | tf_op jit(solution)/shard_map/ppermute | solution.py:62
  358.1 2.2 copy-start.7
  358.1 2.2 copy-start.6
Sparse Core Ops, SparseCore 0:
  360.4 113.8 all-reduce.2
